TPU v7x, 256 devices: a whole 4x4x8 slice. The times are simulated.
256 devices in a mesh: gx: 32 (over z_hi, x, core), gy: 8 (over z_lo, y).
Axes of the slice: x: 4, y: 4, z: 8 (z_hi: 4, z_lo: 2; z = z_hi * 2 + z_lo), core: 2. Of those that a mesh axis runs over, the one named last changes fastest.
Arguments:
- checkpoint: float32 [19, 256, 2048], P(None, 'gx', 'gy'), as said below
- cotangent: float32 [19, 256, 2048], P(None, 'gx', 'gy'), may hold values from -6 to 6
- blade_area: float32 [1536], replicated, may hold values from 0.5 to 2
- hub_tile: int32 [16], replicated, may hold values from 0 to 255
- point_side: int32 [1536], replicated, may hold values from 0 to 8
- point_local: int32 [1536], replicated, may hold values from 0 to 2047
Outputs:
- grad_checkpoint: float32 [19, 256, 2048], P(None, 'gx', 'gy')
- grad_area: float32 [1536], replicated
Inputs may be any that keep to these rules, and one draw needn't show every extreme that they name: `hub_tile`: tile ids count every tile of the slab. `point_side`: every actuator point lies in its hub tile or one of the eight tiles around it. `checkpoint`: populations are positive and near a local equilibrium with density near one and streamwise velocity near 0.08.
All inputs are finite; a program needn't handle non-finite values.
Results may differ from a plain program's by a relative error of at most 0.0003.
Values sent between devices are 32-bit elements; how exact they have to be, the bound alone decides.
No kernel may reach another device: no remote copies, remote signals or barrier semaphores. Data moves between devices by JAX's collectives and lax.ppermute only.
A program may use at most 128 MiB of HBM per device.

v0:
```python
import jax
import jax.numpy as jnp
import numpy as np
from jax import lax
from jax.sharding import PartitionSpec as P

NZ = 16
STEPS = 4
NTURB = 16
PTS = 96
TAU_ZERO = 0.52
SMAGORINSKY = 0.17 * 0.17
TINY = 1e-10
THRUST = 4.0
GHOST_RATES = np.array([1.05, 1.15, 1.25, 1.35, 1.45, 1.55, 1.65, 1.75, 1.85])


def extended(value, sides, width):
    for axis, dim in sides:
        size, length = (lax.axis_size(axis), value.shape[dim])
        up = [(i, (i + 1) % size) for i in range(size)]
        down = [(j, i) for i, j in up]
        last = lax.slice_in_dim(value, length - width, length, axis=dim)
        first = lax.slice_in_dim(value, 0, width, axis=dim)
        before = lax.ppermute(last, axis, up)
        after = lax.ppermute(first, axis, down)
        value = jnp.concatenate([before, value, after], axis=dim)
    return value


def lattice():
    axis_part = [(1, 0, 0), (-1, 0, 0), (0, 1, 0), (0, -1, 0), (0, 0, 1), (0, 0, -1)]
    edge_part = [
        (1, 1, 0),
        (-1, -1, 0),
        (1, -1, 0),
        (-1, 1, 0),
        (1, 0, 1),
        (-1, 0, -1),
        (1, 0, -1),
        (-1, 0, 1),
        (0, 1, 1),
        (0, -1, -1),
        (0, 1, -1),
        (0, -1, 1),
    ]
    vectors = np.array([(0, 0, 0)] + axis_part + edge_part) * 1.0
    weights = np.array([1.0 / 3.0] + [1.0 / 18.0] * 6 + [1.0 / 36.0] * 12)
    opposite = np.array(
        [int(np.argmin(np.abs(vectors + vectors[column]).sum(1))) for column in range(19)]
    )
    return (vectors, weights, opposite)


def orthonormal(monomials, weights):
    rows = []
    for entry in monomials:
        vector = entry * 1.0
        for sweep in range(2):
            for other in rows:
                vector = vector - np.sum(weights * vector * other) * other
        vector = vector / np.sqrt(np.sum(weights * vector * vector))
        rows.append(vector)
    return np.stack(rows, 0)


def tables():
    vectors, weights, opposite = lattice()
    along_x, along_y, along_z = (vectors[:, 0], vectors[:, 1], vectors[:, 2])
    monomials = [
        np.ones(19),
        along_x,
        along_y,
        along_z,
        along_x * along_x,
        along_y * along_y,
        along_z * along_z,
        along_x * along_y,
        along_x * along_z,
        along_y * along_z,
        along_x * along_y * along_y,
        along_x * along_z * along_z,
        along_y * along_x * along_x,
        along_y * along_z * along_z,
        along_z * along_x * along_x,
        along_z * along_y * along_y,
        along_x * along_x * along_y * along_y,
        along_x * along_x * along_z * along_z,
        along_y * along_y * along_z * along_z,
    ]
    basis = orthonormal(monomials, weights)
    second = weights[:, None] * basis[4:10].T
    ghost = weights[:, None] * basis[10:].T * GHOST_RATES[None, :]
    stress = np.stack(
        [
            along_x * along_x,
            along_y * along_y,
            along_z * along_z,
            along_x * along_y,
            along_x * along_z,
            along_y * along_z,
        ],
        0,
    )
    push = 3.0 * weights * along_x
    return {
        "vectors": vectors,
        "weights": weights,
        "opposite": opposite,
        "high": jnp.asarray(basis[4:], jnp.float32),
        "second": jnp.asarray(second, jnp.float32),
        "ghost": jnp.asarray(ghost, jnp.float32),
        "stress": jnp.asarray(stress, jnp.float32),
        "push": jnp.asarray(push, jnp.float32),
        "velt": jnp.asarray(vectors.T, jnp.float32),
        "wvec": jnp.asarray(weights, jnp.float32),
        "vecs": jnp.asarray(vectors, jnp.float32),
    }


def streamwise_velocity(flat, table):
    density = jnp.sum(flat, 0)
    momentum = jnp.dot(table["velt"], flat, precision=lax.Precision.HIGHEST)
    return momentum[0] / density


def collide(flat, force, table):
    density = jnp.sum(flat, 0)
    momentum = jnp.dot(table["velt"], flat, precision=lax.Precision.HIGHEST)
    velocity = momentum / density[None, :]
    project = jnp.dot(table["vecs"], velocity, precision=lax.Precision.HIGHEST)
    speed_sq = jnp.sum(velocity * velocity, 0)
    equil = (
        table["wvec"][:, None]
        * density[None, :]
        * (1.0 + 3.0 * project + 4.5 * project * project - 1.5 * speed_sq[None, :])
    )
    noneq = flat - equil
    stress = jnp.dot(table["stress"], noneq, precision=lax.Precision.HIGHEST)
    square = jnp.sum(stress[:3] * stress[:3], 0) + 2.0 * jnp.sum(stress[3:] * stress[3:], 0)
    relax_time = 0.5 * (
        TAU_ZERO
        + jnp.sqrt(TAU_ZERO * TAU_ZERO + 18.0 * SMAGORINSKY * jnp.sqrt(square + TINY) / density)
    )
    moments = jnp.dot(table["high"], noneq, precision=lax.Precision.HIGHEST)
    relaxed = jnp.dot(
        table["second"], moments[:6] / relax_time[None, :], precision=lax.Precision.HIGHEST
    )
    relaxed = relaxed + jnp.dot(table["ghost"], moments[6:], precision=lax.Precision.HIGHEST)
    return flat - relaxed + table["push"][:, None] * force[None, :]


def wall_mask(vectors, depth):
    keep = np.ones((19, depth))
    for column in range(19):
        if vectors[column, 2] > 0.5:
            keep[column, 0] = 0.0
        if vectors[column, 2] < -0.5:
            keep[column, depth - 1] = 0.0
    return keep


def neighbours(field, vectors, direction):
    pops, width_x, span = field.shape
    depth = NZ
    width_y = span // depth
    step_x = [int(direction * vectors[column, 0]) for column in range(19)]
    step_y = [int(direction * vectors[column, 1]) for column in range(19)]
    step_z = [int(direction * vectors[column, 2]) for column in range(19)]
    padded = extended(field.reshape(pops, width_x, width_y, depth), (("gx", 1), ("gy", 2)), 1)
    padded = padded.reshape(pops, width_x + 2, (width_y + 2) * depth)
    padded = jnp.pad(padded, ((0, 0), (0, 0), (1, 1)))
    pieces = []
    for column in range(19):
        start_x = 1 - step_x[column]
        start_j = depth + 1 - step_y[column] * depth - step_z[column]
        pieces.append(padded[column, start_x : start_x + width_x, start_j : start_j + span])
    return jnp.stack(pieces, 0)


def turbine_total(partial_value):
    return lax.psum(partial_value, ("gx", "gy"))


def body(checkpoint, cotangent, blade_area, hub_tile, point_side, point_local):
    table = tables()
    vectors = table["vectors"]
    opposite = table["opposite"]
    pops, width_x, span = checkpoint.shape
    width_y = span // NZ
    cells = width_x * span
    keep = jnp.asarray(np.tile(wall_mask(vectors, NZ), (1, width_y)), jnp.float32)[:, None, :]
    count_x = lax.axis_size("gx")
    count_y = lax.axis_size("gy")
    index_x = lax.axis_index("gx")
    index_y = lax.axis_index("gy")
    turbine = jnp.arange(NTURB * PTS, dtype=jnp.int32) // PTS
    hub_x = hub_tile // count_y
    hub_y = hub_tile % count_y
    tile_x = (hub_x[turbine] + point_side // 3 - 1) % count_x
    tile_y = (hub_y[turbine] + point_side % 3 - 1) % count_y
    mine = ((tile_x == index_x) & (tile_y == index_y)).astype(jnp.float32)
    denom = jnp.sum(blade_area.reshape(NTURB, PTS), 1)

    def stream_adjoint(adjoint):
        pushed = neighbours(adjoint * keep, vectors, -1)
        return pushed + ((1.0 - keep) * adjoint)[opposite]

    def collide_local(flat, force):
        return collide(flat, force, table)

    def velocity_local(flat):
        return streamwise_velocity(flat, table)

    field = checkpoint
    saved = []
    for counter in range(STEPS):
        flat = (neighbours(field, vectors, 1) * keep + (1.0 - keep) * field[opposite]).reshape(
            pops, cells
        )
        sampled = velocity_local(flat)[point_local] * mine
        numer = turbine_total(jnp.sum((blade_area * sampled).reshape(NTURB, PTS), 1))
        rotor = numer / denom
        thrust = -THRUST * blade_area * rotor[turbine] * sampled
        force = jnp.zeros((cells,), jnp.float32).at[point_local].add(thrust)
        saved.append((flat, sampled, rotor, force))
        field = collide_local(flat, force).reshape(pops, width_x, span)
    adjoint = cotangent
    area_grad = jnp.zeros_like(blade_area)
    for counter in range(STEPS - 1, -1, -1):
        flat, sampled, rotor, force = saved[counter]
        unused, pullback = jax.vjp(collide_local, flat, force)
        flat_bar, force_bar = pullback(adjoint.reshape(pops, cells))
        thrust_bar = force_bar[point_local] * mine
        rotor_here = rotor[turbine]
        sample_bar = thrust_bar * -THRUST * blade_area * rotor_here
        rotor_part = jnp.sum((thrust_bar * -THRUST * blade_area * sampled).reshape(NTURB, PTS), 1)
        rotor_bar = turbine_total(rotor_part)
        numer_bar = rotor_bar / denom
        sample_bar = sample_bar + numer_bar[turbine] * blade_area * mine
        area_grad = area_grad + thrust_bar * -THRUST * rotor_here * sampled
        area_grad = area_grad + mine * rotor_bar[turbine] * (sampled - rotor_here) / denom[turbine]
        speed_bar = jnp.zeros((cells,), jnp.float32).at[point_local].add(sample_bar)
        unused_speed, speed_pull = jax.vjp(velocity_local, flat)
        flat_bar = flat_bar + speed_pull(speed_bar)[0]
        adjoint = stream_adjoint(flat_bar.reshape(pops, width_x, span))
    grad_area = lax.psum(area_grad, ("gx", "gy"))
    return (adjoint, grad_area)


def solution(mesh):
    return jax.shard_map(
        body,
        mesh=mesh,
        in_specs=(P(None, "gx", "gy"), P(None, "gx", "gy"), P(), P(), P(), P()),
        out_specs=(P(None, "gx", "gy"), P()),
        check_vma=False,
    )
```

profile of v0, /device:TPU:1, one launch (start us, length us, event | category | flops | bytes accessed | tf_op | source)
XLA Modules:
  0.0 1147.3 jit_solution(11894280306716798596)
XLA Ops:
  7.4 8.9 select_reduce_fusion.13
  29.9 8.4 gather_fusion.1
  38.4 11.2 fusion.199
  49.9 82.5 %psum.63 = f32[16]{0:T(128)S(1)} all-reduce(f32[16]{0:T(128)S(1)} %reduce_sum.414), channel_id=1, replica_groups=mesh['gx'=32,'gy'=8] {'gx','gy'}, use_global_device_ids=true, to_apply=%region_5.6 | all-reduce | flops 16 | bytes 128 | tf_op jit(solution)/shard_map/psum | solution.py:182
  143.3 8.7 scatter_custom_fusion
  172.3 8.4 gather_fusion.3
  181.3 84.2 %psum.64 = f32[16]{0:T(128)S(1)} all-reduce(f32[16]{0:T(128)S(1)} %reduce_sum.426), channel_id=1, replica_groups=mesh['gx'=32,'gy'=8] {'gx','gy'}, use_global_device_ids=true, to_apply=%region_13.14 | all-reduce | flops 16 | bytes 128 | tf_op jit(solution)/shard_map/psum | solution.py:182
  270.7 5.7 multiply_multiply_fusion.25
  276.4 8.8 scatter_custom_fusion.1
  305.6 8.4 gather_fusion.5
  314.6 84.7 %psum.65 = f32[16]{0:T(128)S(1)} all-reduce(f32[16]{0:T(128)S(1)} %reduce_sum.434), channel_id=1, replica_groups=mesh['gx'=32,'gy'=8] {'gx','gy'}, use_global_device_ids=true, to_apply=%region_20.21 | all-reduce | flops 16 | bytes 128 | tf_op jit(solution)/shard_map/psum | solution.py:182
  404.6 5.7 multiply_multiply_fusion.24
  410.3 8.8 scatter_custom_fusion.2
  421.1 11.7 %gather_fusion.7 = f32[1536]{0:T(1024)} fusion(f32[2048]{0:T(1024)S(1)} %bitcast.826, s32[2048]{0:T(1024)S(1)} %copy-done.21), kind=kCustom, calls=%fused_computation.7 | custom fusion | bytes 18432 | tf_op jit(solution)/shard_map/gather | solution.py:234
  455.5 8.4 gather_fusion.8
  465.3 81.7 %all-reduce.28 = (f32[16]{0:T(128)S(1)}, f32[16]{0:T(128)S(1)}) all-reduce(f32[16]{0:T(128)S(1)} %reduce_sum.455, f32[16]{0:T(128)S(1)} %reduce_sum.454), channel_id=1, replica_groups=mesh['gx'=32,'gy'=8] {'gx','gy'}, use_global_device_ids=true, to_apply=%region_34.35 | all-reduce | flops 32 | bytes 256 | tf_op jit(solution)/shard_map/psum | solution.py:182
  557.5 11.6 %fusion.186 = f32[1536]{0:T(1024)S(1)} fusion(pred[1536]{0:T(1024)(128)(4,1)S(1)} %copy-done.69, f32[1536]{0:T(1024)S(1)} %copy-done.5, pred[1536]{0:T(1024)(128)(4,1)S(1)} %copy-done.76, pred[1536]{0:T(1024)(128)(4,1)S(1)} %copy-done.84, pred[1536]{0:T(1024)(128)(4,1)S(1)} %copy-done.92, pred[1536]{0:T(1024)(128)(4,1)S(1)} %copy-done.100, ...), kind=kLoop, calls=%fused_computation.541 | loop fusion | flops 38400 | bytes 46152 | tf_op jit(solution)/shard_map/add | solution.py:240
  569.1 8.8 scatter_custom_fusion.3
  600.7 8.4 gather_fusion.10
  609.6 80.4 %psum.68 = f32[16]{0:T(128)S(1)} all-reduce(f32[16]{0:T(128)S(1)} %reduce_sum.468), channel_id=1, replica_groups=mesh['gx'=32,'gy'=8] {'gx','gy'}, use_global_device_ids=true, to_apply=%region_42.43 | all-reduce | flops 16 | bytes 128 | tf_op jit(solution)/shard_map/psum | solution.py:182
  697.6 11.3 fusion.184
  708.9 8.8 scatter_custom_fusion.4
  739.8 8.4 gather_fusion.12
  748.6 80.9 %psum.69 = f32[16]{0:T(128)S(1)} all-reduce(f32[16]{0:T(128)S(1)} %reduce_sum.478), channel_id=1, replica_groups=mesh['gx'=32,'gy'=8] {'gx','gy'}, use_global_device_ids=true, to_apply=%region_50.51 | all-reduce | flops 16 | bytes 128 | tf_op jit(solution)/shard_map/psum | solution.py:182
  837.3 11.3 fusion.182
  848.6 8.8 scatter_custom_fusion.5
  879.3 8.4 gather_fusion.14
  888.2 81.0 %psum.70 = f32[16]{0:T(128)S(1)} all-reduce(f32[16]{0:T(128)S(1)} %reduce_sum.491), channel_id=1, replica_groups=mesh['gx'=32,'gy'=8] {'gx','gy'}, use_global_device_ids=true, to_apply=%region_58.59 | all-reduce | flops 16 | bytes 128 | tf_op jit(solution)/shard_map/psum | solution.py:182
  977.0 11.2 fusion.180
  988.2 8.8 scatter_custom_fusion.6
  1009.5 50.7 %fusion.166 = f32[1536]{0:T(1024)S(1)} fusion(pred[1536]{0:T(1024)(128)(4,1)S(1)} %copy-done.72, pred[1536]{0:T(1024)(128)(4,1)S(1)} %copy-done.80, pred[1536]{0:T(1024)(128)(4,1)S(1)} %copy-done.88, pred[1536]{0:T(1024)(128)(4,1)S(1)} %copy-done.96, pred[1536]{0:T(1024)(128)(4,1)S(1)} %copy-done.104, pred[1536]{0:T(1024)(128)(4,1)S(1)} %copy-done.112, ...), kind=kLoop, calls=%fused_computation.513 | loop fusion | flops 190464 | bytes 126276 | tf_op jit(solution)/shard_map/add | solution.py:242
  1061.0 80.0 %psum.71 = f32[1536]{0:T(1024)} all-reduce(f32[1536]{0:T(1024)S(1)} %fusion.166), channel_id=1, replica_groups=mesh['gx'=32,'gy'=8] {'gx','gy'}, use_global_device_ids=true, to_apply=%region_60.61 | all-reduce | flops 1536 | bytes 12288 | tf_op jit(solution)/shard_map/psum | solution.py:247
  (1184 shorter events, 224.9 us)
Async XLA Ops:
  2.0 14.3 %collective-permute-start = (f32[19,1,16,16]{3,2,1,0:T(8,128)S(1)}, f32[19,1,16,16]{3,2,1,0:T(8,128)S(1)}, u32[]{:S(2)}, u32[]{:S(2)}) collective-permute-start(f32[19,1,16,16]{3,2,1,0:T(8,128)S(1)} %get-tuple-element.69), channel_id=1, source_target_pairs={{0,8},{8,16},{16,24},{24,32},{32,40},{40,48},{48,56},{56,64},{64,7... | collective-permute-start | bytes 58376 | tf_op jit(solution)/shard_map/ppermute | solution.py:25
  4.7 11.8 %collective-permute-start.1 = (f32[19,1,16,16]{3,2,1,0:T(8,128)S(1)}, f32[19,1,16,16]{3,2,1,0:T(8,128)S(1)}, u32[]{:S(2)}, u32[]{:S(2)}) collective-permute-start(f32[19,1,16,16]{3,2,1,0:T(8,128)S(1)} %get-tuple-element.68), channel_id=1, source_target_pairs={{8,0},{16,8},{24,16},{32,24},{40,32},{48,40},{56,48},{64,56},{72,6... | collective-permute-start | bytes 58376 | tf_op jit(solution)/shard_map/ppermute | solution.py:26
  17.8 5.6 collective-permute-start.2
  18.5 5.0 collective-permute-start.3
  153.5 2.6 collective-permute-start.4
  153.9 4.7 collective-permute-start.5
  158.8 6.6 collective-permute-start.6
  159.3 6.1 collective-permute-start.7
  286.4 2.3 collective-permute-start.8
  287.4 4.7 collective-permute-start.9
  292.2 6.5 collective-permute-start.10
  293.3 5.4 collective-permute-start.11
  420.3 13.6 %collective-permute-start.12 = (f32[19,1,16,16]{3,2,1,0:T(8,128)S(1)}, f32[19,1,16,16]{3,2,1,0:T(8,128)S(1)}, u32[]{:S(2)}, u32[]{:S(2)}) collective-permute-start(f32[19,1,16,16]{3,2,1,0:T(8,128)S(1)} %get-tuple-element.63), channel_id=1, source_target_pairs={{0,8},{8,16},{16,24},{24,32},{32,40},{40,48},{48,56},{56,64},{64,7... | collective-permute-start | bytes 58376 | tf_op jit(solution)/shard_map/ppermute | solution.py:25
  432.8 4.7 collective-permute-start.13
  438.8 10.4 collective-permute-start.14
  439.3 9.9 collective-permute-start.15
  579.7 3.6 collective-permute-start.16
  581.2 4.7 collective-permute-start.17
  586.0 9.1 collective-permute-start.18
  586.1 9.0 collective-permute-start.19
  719.5 3.4 collective-permute-start.20
  720.7 4.7 collective-permute-start.21
  725.5 8.8 collective-permute-start.22
  725.6 8.7 collective-permute-start.23
  859.2 3.1 collective-permute-start.24
  860.1 4.7 collective-permute-start.25
  865.0 8.9 collective-permute-start.26
  865.0 8.8 collective-permute-start.27
  999.1 6.4 collective-permute-start.28
  1000.1 5.3 collective-permute-start.29
  1005.7 135.3 %collective-permute-start.30 = (f32[19,10,1,16]{3,2,1,0:T(1,128)S(1)}, f32[19,10,1,16]{3,2,1,0:T(1,128)S(1)}, u32[]{:S(2)}, u32[]{:S(2)}) collective-permute-start(f32[19,10,1,16]{3,2,1,0:T(1,128)S(1)} %get-tuple-element.38), channel_id=1, source_target_pairs={{0,1},{1,2},{2,3},{3,4},{4,5},{5,6},{6,7},{7,0},{8,9},{9,10},{10,1... | collective-permute-start | bytes 36488 | tf_op jit(solution)/shard_map/ppermute | solution.py:25
  1005.9 135.1 %collective-permute-start.31 = (f32[19,10,1,16]{3,2,1,0:T(1,128)S(1)}, f32[19,10,1,16]{3,2,1,0:T(1,128)S(1)}, u32[]{:S(2)}, u32[]{:S(2)}) collective-permute-start(f32[19,10,1,16]{3,2,1,0:T(1,128)S(1)} %get-tuple-element.39), channel_id=1, source_target_pairs={{1,0},{2,1},{3,2},{4,3},{5,4},{6,5},{7,6},{0,7},{9,8},{10,9},{11,1... | collective-permute-start | bytes 36488 | tf_op jit(solution)/shard_map/ppermute | solution.py:26
  (275 other events, 11672.1 us)
where the time goes:
time: 1160 us; the launch traced here: 1150 us
  blocking collectives  655 us (56%)
  other arithmetic  277 us (24%)
  local copies, waits for them, and re-layouts  125 us (11%)
  starting transfers between devices  41.8 us (4%)
  waiting for transfers between devices  23 us (2%)
  matrix products  17.3 us (1%)
    psum x7, blocking collectives, turbine_total(): return lax.psum(partial_value, ('gx', 'gy'))  575 us
    psum x1, blocking collectives, body(): grad_area = lax.psum(area_grad, ('gx', 'gy'))  80 us
    add x1, other arithmetic, body(): area_grad + mine * rotor_bar[turbine] * (sampled - rotor_here) / denom[tu...  50.7 us
    add x4, other arithmetic, body(): sample_bar = sample_bar + numer_bar[turbine] * blade_area * mine  45.4 us
    gather x4, local copies, waits for them, and re-layouts, body(): thrust_bar = force_bar[point_local] * mine  36.9 us
    scatter-add x4, other arithmetic, body(): speed_bar = jnp.zeros((cells,), jnp.float32).at[point_local].add(sample_bar)  35.2 us
    gather x4, local copies, waits for them, and re-layouts, body(): sampled = velocity_local(flat)[point_local] * mine  33.6 us
    ppermute x16, starting transfers between devices, extended(): after = lax.ppermute(first, axis, down)  30.8 us
  transfers between devices with their start and end apart: 32, of which 14 were waited for; matrix products, arithmetic and copies ran while one was open for 10% of the time, Pallas kernels for 0%

commit v1 on v0

--- a/solution.py
+++ b/solution.py
@@ -1,3 +1,4 @@
+import functools
 import jax
 import jax.numpy as jnp
 import numpy as np
@@ -13,6 +14,15 @@
 TINY = 1e-10
 THRUST = 4.0
 GHOST_RATES = np.array([1.05, 1.15, 1.25, 1.35, 1.45, 1.55, 1.65, 1.75, 1.85])
+
+
+def create_the_patch(q_in, ax_name, along_axis):
+    wide_out = lax.psum(q_in, ax_name)
+    frame_out = lax.psum(wide_out, along_axis)
+    return frame_out
+
+
+lead_types = functools.partial(create_the_patch, ax_name="gy", along_axis="gx")
 
 
 def extended(value, sides, width):
@@ -179,7 +189,7 @@
 
 
 def turbine_total(partial_value):
-    return lax.psum(partial_value, ("gx", "gy"))
+    return lead_types(partial_value)
 
 
 def body(checkpoint, cotangent, blade_area, hub_tile, point_side, point_local):

time: 1160 us -> 1240 us (1.069)
  blocking collectives: 655 us -> 745 us
    psum x7 -> x14, blocking collectives: 575 us -> 664 us  [the longest x7 565 us: create_the_patch(): frame_out = lax.psum(wide_out, along_axis)]
  transfers between devices with their start and end apart: 32 -> 32, of which waited for: 14 -> 10; matrix products, arithmetic and copies ran while one was open for 10% -> 9% of each run, Pallas kernels for 0% -> 0%
where the time goes in v1:
time: 1240 us; the launch traced here: 1230 us
  blocking collectives  745 us (60%)
  other arithmetic  276 us (22%)
  local copies, waits for them, and re-layouts  125 us (10%)
  starting transfers between devices  46.1 us (4%)
  matrix products  17.3 us (1%)
  waiting for transfers between devices  14.9 us (1%)
    psum x7, blocking collectives, create_the_patch(): frame_out = lax.psum(wide_out, along_axis)  565 us
    psum x7, blocking collectives, create_the_patch(): wide_out = lax.psum(q_in, ax_name)  99.2 us
    psum x1, blocking collectives, body(): grad_area = lax.psum(area_grad, ('gx', 'gy'))  80.3 us
    add x1, other arithmetic, body(): area_grad + mine * rotor_bar[turbine] * (sampled - rotor_here) / denom[tu...  50.4 us
    add x4, other arithmetic, body(): sample_bar = sample_bar + numer_bar[turbine] * blade_area * mine  44.9 us
    ppermute x16, starting transfers between devices, extended(): after = lax.ppermute(first, axis, down)  39.2 us
    gather x4, local copies, waits for them, and re-layouts, body(): thrust_bar = force_bar[point_local] * mine  36.9 us
    scatter-add x4, other arithmetic, body(): speed_bar = jnp.zeros((cells,), jnp.float32).at[point_local].add(sample_bar)  35.2 us
  transfers between devices with their start and end apart: 32, of which 10 were waited for; matrix products, arithmetic and copies ran while one was open for 9% of the time, Pallas kernels for 0%

profile of v1, /device:TPU:1, one launch (start us, length us, event | category | flops | bytes accessed | tf_op | source)
XLA Modules:
  0.0 1231.5 jit_solution(56798369825196747)
XLA Ops:
  7.5 8.8 select_reduce_fusion.13
  29.9 8.4 gather_fusion.1
  38.4 11.3 fusion.199
  49.9 16.0 %psum.119 = f32[16]{0:T(128)S(1)} all-reduce(f32[16]{0:T(128)S(1)} %reduce_sum.414), channel_id=1, replica_groups=mesh['gx'=32,'gy'=8] {'gy'}, use_global_device_ids=true, to_apply=%region_5.6 | all-reduce | flops 16 | bytes 128 | tf_op jit(solution)/shard_map/psum | solution.py:20
  65.9 80.6 %psum.120 = f32[16]{0:T(128)S(1)} all-reduce(f32[16]{0:T(128)S(1)} %psum.119), channel_id=1, replica_groups=mesh['gx'=32,'gy'=8] {'gx'}, use_global_device_ids=true, to_apply=%region_6.7 | all-reduce | flops 16 | bytes 128 | tf_op jit(solution)/shard_map/psum | solution.py:21
  157.4 8.7 scatter_custom_fusion
  194.3 16.1 %psum.121 = f32[16]{0:T(128)S(1)} all-reduce(f32[16]{0:T(128)S(1)} %reduce_sum.426), channel_id=1, replica_groups=mesh['gx'=32,'gy'=8] {'gy'}, use_global_device_ids=true, to_apply=%region_14.15 | all-reduce | flops 16 | bytes 128 | tf_op jit(solution)/shard_map/psum | solution.py:20
  210.5 80.8 %psum.122 = f32[16]{0:T(128)S(1)} all-reduce(f32[16]{0:T(128)S(1)} %psum.121), channel_id=1, replica_groups=mesh['gx'=32,'gy'=8] {'gx'}, use_global_device_ids=true, to_apply=%region_15.16 | all-reduce | flops 16 | bytes 128 | tf_op jit(solution)/shard_map/psum | solution.py:21
  302.1 8.8 scatter_custom_fusion.1
  331.8 8.4 gather_fusion.5
  340.5 15.4 %psum.123 = f32[16]{0:T(128)S(1)} all-reduce(f32[16]{0:T(128)S(1)} %reduce_sum.434), channel_id=1, replica_groups=mesh['gx'=32,'gy'=8] {'gy'}, use_global_device_ids=true, to_apply=%region_22.23 | all-reduce | flops 16 | bytes 128 | tf_op jit(solution)/shard_map/psum | solution.py:20
  355.9 81.3 %psum.124 = f32[16]{0:T(128)S(1)} all-reduce(f32[16]{0:T(128)S(1)} %psum.123), channel_id=1, replica_groups=mesh['gx'=32,'gy'=8] {'gx'}, use_global_device_ids=true, to_apply=%region_23.24 | all-reduce | flops 16 | bytes 128 | tf_op jit(solution)/shard_map/psum | solution.py:21
  448.1 8.8 scatter_custom_fusion.2
  458.9 11.8 gather_fusion.7
  503.3 12.5 %all-reduce.29 = (f32[16]{0:T(128)S(1)}, f32[16]{0:T(128)S(1)}) all-reduce(f32[16]{0:T(128)S(1)} %reduce_sum.455, f32[16]{0:T(128)S(1)} %reduce_sum.454), channel_id=1, replica_groups=mesh['gx'=32,'gy'=8] {'gy'}, use_global_device_ids=true, to_apply=%region_38.39 | all-reduce | flops 32 | bytes 256 | tf_op jit(solution)/shard_map/psum | solution.py:20
  515.8 79.2 %all-reduce.28 = (f32[16]{0:T(128)S(1)}, f32[16]{0:T(128)S(1)}) all-reduce(f32[16]{0:T(128)S(1)} %get-tuple-element.20, f32[16]{0:T(128)S(1)} %get-tuple-element.21), channel_id=1, replica_groups=mesh['gx'=32,'gy'=8] {'gx'}, use_global_device_ids=true, to_apply=%region_39.40 | all-reduce | flops 32 | bytes 256 | tf_op jit(solution)/shard_map/psum | solution.py:21
  605.2 11.3 fusion.186
  616.5 8.8 scatter_custom_fusion.3
  655.2 13.1 %psum.129 = f32[16]{0:T(128)S(1)} all-reduce(f32[16]{0:T(128)S(1)} %reduce_sum.468), channel_id=1, replica_groups=mesh['gx'=32,'gy'=8] {'gy'}, use_global_device_ids=true, to_apply=%region_47.48 | all-reduce | flops 16 | bytes 128 | tf_op jit(solution)/shard_map/psum | solution.py:20
  668.3 81.8 %psum.130 = f32[16]{0:T(128)S(1)} all-reduce(f32[16]{0:T(128)S(1)} %psum.129), channel_id=1, replica_groups=mesh['gx'=32,'gy'=8] {'gx'}, use_global_device_ids=true, to_apply=%region_48.49 | all-reduce | flops 16 | bytes 128 | tf_op jit(solution)/shard_map/psum | solution.py:21
  757.7 11.3 fusion.184
  769.0 8.8 scatter_custom_fusion.4
  807.7 13.0 %psum.131 = f32[16]{0:T(128)S(1)} all-reduce(f32[16]{0:T(128)S(1)} %reduce_sum.478), channel_id=1, replica_groups=mesh['gx'=32,'gy'=8] {'gy'}, use_global_device_ids=true, to_apply=%region_56.57 | all-reduce | flops 16 | bytes 128 | tf_op jit(solution)/shard_map/psum | solution.py:20
  820.8 80.8 %psum.132 = f32[16]{0:T(128)S(1)} all-reduce(f32[16]{0:T(128)S(1)} %psum.131), channel_id=1, replica_groups=mesh['gx'=32,'gy'=8] {'gx'}, use_global_device_ids=true, to_apply=%region_57.58 | all-reduce | flops 16 | bytes 128 | tf_op jit(solution)/shard_map/psum | solution.py:21
  909.2 11.2 fusion.182
  920.4 8.8 scatter_custom_fusion.5
  959.2 13.0 %psum.133 = f32[16]{0:T(128)S(1)} all-reduce(f32[16]{0:T(128)S(1)} %reduce_sum.491), channel_id=1, replica_groups=mesh['gx'=32,'gy'=8] {'gy'}, use_global_device_ids=true, to_apply=%region_65.66 | all-reduce | flops 16 | bytes 128 | tf_op jit(solution)/shard_map/psum | solution.py:20
  972.2 80.7 %psum.134 = f32[16]{0:T(128)S(1)} all-reduce(f32[16]{0:T(128)S(1)} %psum.133), channel_id=1, replica_groups=mesh['gx'=32,'gy'=8] {'gx'}, use_global_device_ids=true, to_apply=%region_66.67 | all-reduce | flops 16 | bytes 128 | tf_op jit(solution)/shard_map/psum | solution.py:21
  1060.6 11.1 fusion.180
  1071.7 8.8 scatter_custom_fusion.6
  1093.7 50.4 %fusion.166 = f32[1536]{0:T(1024)S(1)} fusion(pred[1536]{0:T(1024)(128)(4,1)S(1)} %copy-done.73, pred[1536]{0:T(1024)(128)(4,1)S(1)} %copy-done.81, pred[1536]{0:T(1024)(128)(4,1)S(1)} %copy-done.89, pred[1536]{0:T(1024)(128)(4,1)S(1)} %copy-done.97, pred[1536]{0:T(1024)(128)(4,1)S(1)} %copy-done.105, pred[1536]{0:T(1024)(128)(4,1)S(1)} %copy-done.113, ...), kind=kLoop, calls=%fused_computation.513 | loop fusion | flops 190464 | bytes 126276 | tf_op jit(solution)/shard_map/add | solution.py:252
  1144.8 80.3 %psum.135 = f32[1536]{0:T(1024)} all-reduce(f32[1536]{0:T(1024)S(1)} %fusion.166), channel_id=1, replica_groups=mesh['gx'=32,'gy'=8] {'gx','gy'}, use_global_device_ids=true, to_apply=%region_68.69 | all-reduce | flops 1536 | bytes 12288 | tf_op jit(solution)/shard_map/psum | solution.py:257
  (1193 shorter events, 273.6 us)
Async XLA Ops:
  2.0 14.3 %collective-permute-start = (f32[19,1,16,16]{3,2,1,0:T(8,128)S(1)}, f32[19,1,16,16]{3,2,1,0:T(8,128)S(1)}, u32[]{:S(2)}, u32[]{:S(2)}) collective-permute-start(f32[19,1,16,16]{3,2,1,0:T(8,128)S(1)} %get-tuple-element.71), channel_id=1, source_target_pairs={{0,8},{8,16},{16,24},{24,32},{32,40},{40,48},{48,56},{56,64},{64,7... | collective-permute-start | bytes 58376 | tf_op jit(solution)/shard_map/ppermute | solution.py:35
  4.7 11.8 collective-permute-start.1
  17.8 5.6 collective-permute-start.2
  18.4 5.0 collective-permute-start.3
  167.6 2.3 collective-permute-start.4
  167.6 4.9 collective-permute-start.5
  172.7 5.6 collective-permute-start.6
  172.8 5.6 collective-permute-start.7
  312.1 2.9 collective-permute-start.8
  313.2 4.7 collective-permute-start.9
  318.0 6.5 collective-permute-start.10
  318.1 6.5 collective-permute-start.11
  458.1 14.2 %collective-permute-start.12 = (f32[19,1,16,16]{3,2,1,0:T(8,128)S(1)}, f32[19,1,16,16]{3,2,1,0:T(8,128)S(1)}, u32[]{:S(2)}, u32[]{:S(2)}) collective-permute-start(f32[19,1,16,16]{3,2,1,0:T(8,128)S(1)} %get-tuple-element.65), channel_id=1, source_target_pairs={{0,8},{8,16},{16,24},{24,32},{32,40},{40,48},{48,56},{56,64},{64,7... | collective-permute-start | bytes 58376 | tf_op jit(solution)/shard_map/ppermute | solution.py:35
  470.7 4.7 collective-permute-start.13
  476.6 10.6 collective-permute-start.14
  476.7 10.5 collective-permute-start.15
  627.1 4.3 collective-permute-start.16
  627.2 4.7 collective-permute-start.17
  632.1 8.7 collective-permute-start.18
  633.7 7.1 collective-permute-start.19
  779.6 3.4 collective-permute-start.20
  779.7 4.7 collective-permute-start.21
  784.6 8.8 collective-permute-start.22
  784.7 8.7 collective-permute-start.23
  931.0 3.3 collective-permute-start.24
  931.1 4.7 collective-permute-start.25
  936.0 8.9 collective-permute-start.26
  936.1 8.8 collective-permute-start.27
  1082.5 7.0 collective-permute-start.28
  1082.6 7.0 collective-permute-start.29
  1089.8 135.3 %collective-permute-start.30 = (f32[19,10,1,16]{3,2,1,0:T(1,128)S(1)}, f32[19,10,1,16]{3,2,1,0:T(1,128)S(1)}, u32[]{:S(2)}, u32[]{:S(2)}) collective-permute-start(f32[19,10,1,16]{3,2,1,0:T(1,128)S(1)} %get-tuple-element.40), channel_id=1, source_target_pairs={{0,1},{1,2},{2,3},{3,4},{4,5},{5,6},{6,7},{7,0},{8,9},{9,10},{10,1... | collective-permute-start | bytes 36488 | tf_op jit(solution)/shard_map/ppermute | solution.py:35
  1090.8 134.2 %collective-permute-start.31 = (f32[19,10,1,16]{3,2,1,0:T(1,128)S(1)}, f32[19,10,1,16]{3,2,1,0:T(1,128)S(1)}, u32[]{:S(2)}, u32[]{:S(2)}) collective-permute-start(f32[19,10,1,16]{3,2,1,0:T(1,128)S(1)} %get-tuple-element.41), channel_id=1, source_target_pairs={{1,0},{2,1},{3,2},{4,3},{5,4},{6,5},{7,6},{0,7},{9,8},{10,9},{11,1... | collective-permute-start | bytes 36488 | tf_op jit(solution)/shard_map/ppermute | solution.py:36
  (276 other events, 13059.1 us)
